TPU v7x, 32 devices: a whole 2x2x4 slice. The times are simulated.
32 devices in a mesh: obs: 8 (over y, x, core), rows: 4 (over z).
Axes of the slice: x: 2, y: 2, z: 4, core: 2. Of those that a mesh axis runs over, the one named last changes fastest.
Arguments:
- state: float32 [8192, 256], P(('obs', 'rows')), may hold values from -6 to 6
- foot_tiles: int32 [192, 4], P('obs'), may hold values from 0 to 3
- foot_weight: float32 [192, 4, 256], P('obs'), may hold values from -0.25 to 0.25
- azimuth: float32 [768], P('obs'), may hold values from -3.140625 to 3.140625
- obs_value: float32 [768], replicated, may hold values from 0.5 to 2.5
- obs_var: float32 [768], replicated, may hold values from 0.3 to 3
- tile_bin: int32 [32, 768], P(('obs', 'rows')), may hold values from 0 to 14
- obs_bin: int32 [768, 768], P('obs'), may hold values from 0 to 14
- order: int32 [768], replicated, may hold values from 0 to 767, as said below
Outputs:
- analysis: float32 [8192, 256], P(('obs', 'rows'))
Inputs may be any that keep to these rules, and one draw needn't show every extreme that they name: foot_tiles numbers a tile among the 4 tiles of the footprint's own observation group. `order`: a permutation of the observables; each aligned block of 128 entries is one batch, and every batch holds equally many observables of each observation group (the 96 observables of group g are g * 96 to g * 96 + 95).
All inputs are finite; a program needn't handle non-finite values.
Results may differ from a plain program's by a relative error of at most 0.0003.
Values sent between devices are 32-bit elements; how exact they have to be, the bound alone decides.
A program may use at most 64 MiB of HBM per device.

v0:
```python
import jax
import jax.numpy as jnp
from jax import lax
from jax.sharding import PartitionSpec as P

MEMBERS = 256
BATCH = 128
BATCHES = 6
TILE = 256
RADIUS = 8


HIGH = lax.Precision.HIGHEST


def model_function(east_wind, north_wind, angles):
    speed = jnp.sqrt(east_wind * east_wind + north_wind * north_wind + 1.0)
    cosine = (east_wind * jnp.cos(angles) + north_wind * jnp.sin(angles)) / speed
    return jnp.exp(0.6 * jnp.log(speed)) * (0.7 + 0.4 * cosine + 0.6 * cosine * cosine)


def taper_weight(bins):
    scaled = 1.0 - bins.astype(jnp.float32) / RADIUS
    return jnp.where(bins < RADIUS, scaled * scaled, jnp.zeros_like(scaled))


def batch_gains(batch_obs, values, variances):
    row_mean = jnp.mean(batch_obs, axis=1)
    perturb = batch_obs - row_mean[:, None]
    innov = values - row_mean
    covariance = jnp.dot(perturb, perturb.T, precision=HIGH, preferred_element_type=jnp.float32) / (
        MEMBERS - 1
    ) + jnp.diag(variances)
    factor = jnp.linalg.cholesky(covariance)
    middle = jax.scipy.linalg.solve_triangular(factor, innov, lower=True)
    solved = jax.scipy.linalg.solve_triangular(factor, middle, lower=True, trans=1)
    eye_matrix = jnp.eye(BATCH, dtype=jnp.float32)
    shifted = factor + jnp.diag(jnp.sqrt(variances))
    inverse = jax.scipy.linalg.solve_triangular(shifted, eye_matrix, lower=True)
    gain_matrix = jax.scipy.linalg.solve_triangular(factor, inverse, lower=True, trans=1)
    return (perturb, solved, gain_matrix)


def localised(ensemble, weights, rows_per, perturb, solved, gain_matrix):
    row_mean = jnp.mean(ensemble, axis=1, keepdims=True)
    deviation = ensemble - row_mean
    product = jnp.dot(deviation, perturb.T, precision=HIGH, preferred_element_type=jnp.float32) / (
        MEMBERS - 1
    )
    product = (product.reshape(-1, rows_per, BATCH) * weights[:, None, :]).reshape(product.shape)
    row_mean = row_mean + jnp.dot(
        product, solved[:, None], precision=HIGH, preferred_element_type=jnp.float32
    )
    mixed = jnp.dot(product, gain_matrix, precision=HIGH, preferred_element_type=jnp.float32)
    deviation = deviation - jnp.dot(
        mixed, perturb, precision=HIGH, preferred_element_type=jnp.float32
    )
    return row_mean + deviation


def update_rows(ensemble, weights, rows_per, perturb, solved, gain_matrix):
    return localised(ensemble, weights, rows_per, perturb, solved, gain_matrix)


def shards(state, foot_tiles, foot_weight, azimuth, obs_value, obs_var, tile_bin, obs_bin, order):
    tiles_dev = state.shape[0] // TILE
    half_tile = TILE // 2
    foot_count = foot_tiles.shape[0]
    row_index = lax.axis_index("rows")
    local_tile = foot_tiles - row_index * tiles_dev
    onehot = (
        local_tile[:, :, None] == jnp.arange(tiles_dev, dtype=jnp.int32)[None, None, :]
    ).astype(jnp.float32)
    coefficients = jnp.einsum("ftq,ftc->fqc", onehot, foot_weight, precision=HIGH)
    partial_value = jnp.einsum(
        "fqhc,qhcm->fhm",
        coefficients.reshape(foot_count, tiles_dev, 2, half_tile),
        state.reshape(tiles_dev, 2, half_tile, MEMBERS),
        precision=HIGH,
    )
    wind_sums = lax.psum(partial_value, "rows")
    angles = azimuth.reshape(foot_count, 4)
    group_obs = model_function(
        wind_sums[:, 0, None, :], wind_sums[:, 1, None, :], angles[:, :, None]
    ).reshape(foot_count * 4, MEMBERS)
    every_obs = lax.all_gather(group_obs, "obs", axis=0, tiled=True)
    every_bins = lax.all_gather(obs_bin, "obs", axis=0, tiled=True)
    hold_count = every_obs.shape[0] // lax.axis_size("rows")
    hold_start = row_index * hold_count
    held_obs = lax.dynamic_slice_in_dim(every_obs, hold_start, hold_count, 0)
    held_bins = lax.dynamic_slice_in_dim(every_bins, hold_start, hold_count, 0)
    positions = hold_start + jnp.arange(hold_count, dtype=jnp.int32)

    def batch_step(batch_num, carry):
        ensemble, held = carry
        picked = lax.dynamic_slice_in_dim(order, batch_num * BATCH, BATCH)
        select = (picked[:, None] == positions[None, :]).astype(jnp.float32)
        selected = jnp.dot(select, held, precision=HIGH, preferred_element_type=jnp.float32)
        batch_obs = lax.psum(selected, "rows")
        perturb, solved, gain_matrix = batch_gains(batch_obs, obs_value[picked], obs_var[picked])
        ensemble = update_rows(
            ensemble, taper_weight(tile_bin[:, picked]), TILE, perturb, solved, gain_matrix
        )
        held = update_rows(
            held, taper_weight(held_bins[:, picked]), 1, perturb, solved, gain_matrix
        )
        return (ensemble, held)

    ensemble, held_obs = lax.fori_loop(0, BATCHES, batch_step, (state, held_obs))
    return ensemble


def solution(mesh):
    return jax.shard_map(
        shards,
        mesh=mesh,
        in_specs=(
            P(("obs", "rows"), None),
            P("obs", None),
            P("obs", None, None),
            P("obs"),
            P(),
            P(),
            P(("obs", "rows"), None),
            P("obs", None),
            P(),
        ),
        out_specs=P(("obs", "rows"), None),
        check_vma=False,
    )
```

profile of v0, /device:TPU:0, one launch (start us, length us, event | category | flops | bytes accessed | tf_op | source)
XLA Modules:
  0.0 518.2 jit_solution(12764114591722689384)
XLA Ops:
  9.0 21.3 %psum.18 = f32[24,2,256]{2,0,1:T(8,128)S(1)} all-reduce(f32[24,2,256]{2,0,1:T(8,128)S(1)} %convolution_bitcast_fusion.2), channel_id=1, replica_groups=mesh['obs'=8,'rows'=4] {'rows'}, use_global_device_ids=true, to_apply=%region_0.0 | all-reduce | flops 12288 | bytes 98304 | tf_op jit(solution)/shard_map/psum | solution.py:81
  30.8 12.6 %all_gather.6 = f32[768,256]{1,0:T(8,128)S(1)} all-gather(f32[96,256]{1,0:T(8,128)S(1)} %fusion.37), channel_id=1, replica_groups=mesh['obs'=8,'rows'=4] {'obs'}, dimensions={0}, use_global_device_ids=true | all-gather | bytes 884736 | tf_op jit(solution)/shard_map/all_gather | solution.py:86
  44.9 465.7 %while.16 = (s32[]{:T(128)}, f32[256,256]{1,0:T(8,128)S(1)}, f32[192,256]{1,0:T(8,128)S(1)}, s32[768]{0:T(1024)}, s32[1,768]{1,0:T(1,128)S(1)}, /*index=5*/f32[7...) while((s32[]{:T(128)}, f32[256,256]{1,0:T(8,128)S(1)}, ...), condition=%wide.region_8.9_spmd.clone, body=%wide.region_1.8_spmd.clone.sunk | while | flops 619048640 | bytes 6734617 | solution.py:109
  50.7 32.1 %all-reduce.2.cloned.1.call-done = f32[128,256]{1,0:T(8,128)} async-done(((f32[128,256]{1,0:T(8,128)}), f32[128,256]{1,0:T(8,128)}) %all-reduce.2.cloned.1.call-update) | async-done | bytes 131088 | tf_op jit(solution)/shard_map/while/body/eval_jaxpr/psum | solution.py:99
  85.5 11.7 %cholesky.80 = f32[128,128]{1,0:T(8,128)S(1)} custom-call(f32[128,128]{1,0:T(8,128)S(1)} %fusion.130), custom_call_target="Cholesky" | custom-call | tf_op jit(solution)/shard_map/while/body/eval_jaxpr/jit(cholesky)/cholesky | solution.py:34
  98.6 9.8 %custom-call.49 = f32[1,128,128]{1,2,0:T(8,128)S(1)} custom-call(f32[1,128,128]{2,1,0:T(8,128)S(1)} %get-tuple-element.352), custom_call_target="InvertDiagBlocksLowerTriangular" | custom-call | tf_op jit(solution)/shard_map/while/body/eval_jaxpr/jit(_solve_triangular)/triangular_solve | solution.py:39
  108.7 9.8 %custom-call.50 = f32[1,128,128]{1,2,0:T(8,128)S(1)} custom-call(f32[1,128,128]{2,1,0:T(8,128)S(1)} %get-tuple-element.353), custom_call_target="InvertDiagBlocksLowerTriangular" | custom-call | tf_op jit(solution)/shard_map/while/body/eval_jaxpr/jit(_solve_triangular)/triangular_solve | solution.py:36
  128.7 31.8 %all-reduce.2.cloned.1.call-done = f32[128,256]{1,0:T(8,128)} async-done(((f32[128,256]{1,0:T(8,128)}), f32[128,256]{1,0:T(8,128)}) %all-reduce.2.cloned.1.call-update) | async-done | bytes 131088 | tf_op jit(solution)/shard_map/while/body/eval_jaxpr/psum | solution.py:99
  163.2 11.7 %cholesky.80 = f32[128,128]{1,0:T(8,128)S(1)} custom-call(f32[128,128]{1,0:T(8,128)S(1)} %fusion.130), custom_call_target="Cholesky" | custom-call | tf_op jit(solution)/shard_map/while/body/eval_jaxpr/jit(cholesky)/cholesky | solution.py:34
  176.3 9.8 %custom-call.49 = f32[1,128,128]{1,2,0:T(8,128)S(1)} custom-call(f32[1,128,128]{2,1,0:T(8,128)S(1)} %get-tuple-element.352), custom_call_target="InvertDiagBlocksLowerTriangular" | custom-call | tf_op jit(solution)/shard_map/while/body/eval_jaxpr/jit(_solve_triangular)/triangular_solve | solution.py:39
  186.4 9.8 %custom-call.50 = f32[1,128,128]{1,2,0:T(8,128)S(1)} custom-call(f32[1,128,128]{2,1,0:T(8,128)S(1)} %get-tuple-element.353), custom_call_target="InvertDiagBlocksLowerTriangular" | custom-call | tf_op jit(solution)/shard_map/while/body/eval_jaxpr/jit(_solve_triangular)/triangular_solve | solution.py:36
  206.4 31.5 %all-reduce.2.cloned.1.call-done = f32[128,256]{1,0:T(8,128)} async-done(((f32[128,256]{1,0:T(8,128)}), f32[128,256]{1,0:T(8,128)}) %all-reduce.2.cloned.1.call-update) | async-done | bytes 131088 | tf_op jit(solution)/shard_map/while/body/eval_jaxpr/psum | solution.py:99
  240.6 11.7 %cholesky.80 = f32[128,128]{1,0:T(8,128)S(1)} custom-call(f32[128,128]{1,0:T(8,128)S(1)} %fusion.130), custom_call_target="Cholesky" | custom-call | tf_op jit(solution)/shard_map/while/body/eval_jaxpr/jit(cholesky)/cholesky | solution.py:34
  253.7 9.8 %custom-call.49 = f32[1,128,128]{1,2,0:T(8,128)S(1)} custom-call(f32[1,128,128]{2,1,0:T(8,128)S(1)} %get-tuple-element.352), custom_call_target="InvertDiagBlocksLowerTriangular" | custom-call | tf_op jit(solution)/shard_map/while/body/eval_jaxpr/jit(_solve_triangular)/triangular_solve | solution.py:39
  263.8 9.8 %custom-call.50 = f32[1,128,128]{1,2,0:T(8,128)S(1)} custom-call(f32[1,128,128]{2,1,0:T(8,128)S(1)} %get-tuple-element.353), custom_call_target="InvertDiagBlocksLowerTriangular" | custom-call | tf_op jit(solution)/shard_map/while/body/eval_jaxpr/jit(_solve_triangular)/triangular_solve | solution.py:36
  283.8 31.5 %all-reduce.2.cloned.1.call-done = f32[128,256]{1,0:T(8,128)} async-done(((f32[128,256]{1,0:T(8,128)}), f32[128,256]{1,0:T(8,128)}) %all-reduce.2.cloned.1.call-update) | async-done | bytes 131088 | tf_op jit(solution)/shard_map/while/body/eval_jaxpr/psum | solution.py:99
  317.9 11.7 %cholesky.80 = f32[128,128]{1,0:T(8,128)S(1)} custom-call(f32[128,128]{1,0:T(8,128)S(1)} %fusion.130), custom_call_target="Cholesky" | custom-call | tf_op jit(solution)/shard_map/while/body/eval_jaxpr/jit(cholesky)/cholesky | solution.py:34
  341.1 9.8 %custom-call.50 = f32[1,128,128]{1,2,0:T(8,128)S(1)} custom-call(f32[1,128,128]{2,1,0:T(8,128)S(1)} %get-tuple-element.353), custom_call_target="InvertDiagBlocksLowerTriangular" | custom-call | tf_op jit(solution)/shard_map/while/body/eval_jaxpr/jit(_solve_triangular)/triangular_solve | solution.py:36
  361.2 31.5 %all-reduce.2.cloned.1.call-done = f32[128,256]{1,0:T(8,128)} async-done(((f32[128,256]{1,0:T(8,128)}), f32[128,256]{1,0:T(8,128)}) %all-reduce.2.cloned.1.call-update) | async-done | bytes 131088 | tf_op jit(solution)/shard_map/while/body/eval_jaxpr/psum | solution.py:99
  395.3 11.7 %cholesky.80 = f32[128,128]{1,0:T(8,128)S(1)} custom-call(f32[128,128]{1,0:T(8,128)S(1)} %fusion.130), custom_call_target="Cholesky" | custom-call | tf_op jit(solution)/shard_map/while/body/eval_jaxpr/jit(cholesky)/cholesky | solution.py:34
  418.5 9.8 %custom-call.50 = f32[1,128,128]{1,2,0:T(8,128)S(1)} custom-call(f32[1,128,128]{2,1,0:T(8,128)S(1)} %get-tuple-element.353), custom_call_target="InvertDiagBlocksLowerTriangular" | custom-call | tf_op jit(solution)/shard_map/while/body/eval_jaxpr/jit(_solve_triangular)/triangular_solve | solution.py:36
  438.6 31.8 %all-reduce.2.cloned.1.call-done = f32[128,256]{1,0:T(8,128)} async-done(((f32[128,256]{1,0:T(8,128)}), f32[128,256]{1,0:T(8,128)}) %all-reduce.2.cloned.1.call-update) | async-done | bytes 131088 | tf_op jit(solution)/shard_map/while/body/eval_jaxpr/psum | solution.py:99
  473.0 11.7 %cholesky.80 = f32[128,128]{1,0:T(8,128)S(1)} custom-call(f32[128,128]{1,0:T(8,128)S(1)} %fusion.130), custom_call_target="Cholesky" | custom-call | tf_op jit(solution)/shard_map/while/body/eval_jaxpr/jit(cholesky)/cholesky | solution.py:34
  496.2 9.8 %custom-call.50 = f32[1,128,128]{1,2,0:T(8,128)S(1)} custom-call(f32[1,128,128]{2,1,0:T(8,128)S(1)} %get-tuple-element.353), custom_call_target="InvertDiagBlocksLowerTriangular" | custom-call | tf_op jit(solution)/shard_map/while/body/eval_jaxpr/jit(_solve_triangular)/triangular_solve | solution.py:36
  (278 shorter events, 120.4 us)
Async XLA Ops:
  6.5 1.9 copy-start
  6.5 24.0 %copy-start.6 = (f32[96]{0:T(128)S(1)}, f32[96]{0:T(128)}, u32[]{:S(2)}) copy-start(f32[96]{0:T(128)} %param.14) | copy-start | bytes 1156
  6.5 36.9 %all-gather.2.cloned.1.call-start = ((), (), s32[]{:S(2)}) async-start(), calls=%async_computation | async-start | bytes 2654208 | tf_op jit(solution)/shard_map/all_gather | solution.py:87
  30.5 14.4 %copy-start.1 = (f32[768]{0:T(1024)S(1)}, f32[768]{0:T(1024)}, u32[]{:S(2)}) copy-start(f32[768]{0:T(1024)} %param.16) | copy-start | bytes 9220
  30.5 14.4 %copy-start.2 = (f32[768]{0:T(1024)S(1)}, f32[768]{0:T(1024)}, u32[]{:S(2)}) copy-start(f32[768]{0:T(1024)} %param.15) | copy-start | bytes 9220
  30.5 14.4 %copy-start.5 = (s32[1,768]{1,0:T(1,128)S(1)}, s32[1,768]{1,0:T(1,128)}, u32[]{:S(2)}) copy-start(s32[1,768]{1,0:T(1,128)} %param.17) | copy-start | bytes 9220
  45.1 37.8 %all-reduce.2.cloned.1.call-start = ((), (), s32[]{:S(2)}) async-start(), calls=%async_computation.1 | async-start | bytes 262144 | tf_op jit(solution)/shard_map/while/body/eval_jaxpr/psum | solution.py:99
  82.9 38.1 %copy-start.3 = (f32[128,256]{1,0:T(8,128)S(1)}, f32[128,256]{1,0:T(8,128)}, u32[]{:S(2)}) copy-start(f32[128,256]{1,0:T(8,128)} %all-reduce.2.cloned.1.call-done) | copy-start | bytes 393220 | tf_op jit(solution)/shard_map/while
  123.1 37.5 %all-reduce.2.cloned.1.call-start = ((), (), s32[]{:S(2)}) async-start(), calls=%async_computation.1 | async-start | bytes 262144 | tf_op jit(solution)/shard_map/while/body/eval_jaxpr/psum | solution.py:99
  160.6 38.1 %copy-start.3 = (f32[128,256]{1,0:T(8,128)S(1)}, f32[128,256]{1,0:T(8,128)}, u32[]{:S(2)}) copy-start(f32[128,256]{1,0:T(8,128)} %all-reduce.2.cloned.1.call-done) | copy-start | bytes 393220 | tf_op jit(solution)/shard_map/while
  200.8 37.2 %all-reduce.2.cloned.1.call-start = ((), (), s32[]{:S(2)}) async-start(), calls=%async_computation.1 | async-start | bytes 262144 | tf_op jit(solution)/shard_map/while/body/eval_jaxpr/psum | solution.py:99
  237.9 38.1 %copy-start.3 = (f32[128,256]{1,0:T(8,128)S(1)}, f32[128,256]{1,0:T(8,128)}, u32[]{:S(2)}) copy-start(f32[128,256]{1,0:T(8,128)} %all-reduce.2.cloned.1.call-done) | copy-start | bytes 393220 | tf_op jit(solution)/shard_map/while
  278.2 37.2 %all-reduce.2.cloned.1.call-start = ((), (), s32[]{:S(2)}) async-start(), calls=%async_computation.1 | async-start | bytes 262144 | tf_op jit(solution)/shard_map/while/body/eval_jaxpr/psum | solution.py:99
  315.3 38.1 %copy-start.3 = (f32[128,256]{1,0:T(8,128)S(1)}, f32[128,256]{1,0:T(8,128)}, u32[]{:S(2)}) copy-start(f32[128,256]{1,0:T(8,128)} %all-reduce.2.cloned.1.call-done) | copy-start | bytes 393220 | tf_op jit(solution)/shard_map/while
  355.5 37.2 %all-reduce.2.cloned.1.call-start = ((), (), s32[]{:S(2)}) async-start(), calls=%async_computation.1 | async-start | bytes 262144 | tf_op jit(solution)/shard_map/while/body/eval_jaxpr/psum | solution.py:99
  392.7 38.1 %copy-start.3 = (f32[128,256]{1,0:T(8,128)S(1)}, f32[128,256]{1,0:T(8,128)}, u32[]{:S(2)}) copy-start(f32[128,256]{1,0:T(8,128)} %all-reduce.2.cloned.1.call-done) | copy-start | bytes 393220 | tf_op jit(solution)/shard_map/while
  432.9 37.5 %all-reduce.2.cloned.1.call-start = ((), (), s32[]{:S(2)}) async-start(), calls=%async_computation.1 | async-start | bytes 262144 | tf_op jit(solution)/shard_map/while/body/eval_jaxpr/psum | solution.py:99
  470.4 38.1 %copy-start.3 = (f32[128,256]{1,0:T(8,128)S(1)}, f32[128,256]{1,0:T(8,128)}, u32[]{:S(2)}) copy-start(f32[128,256]{1,0:T(8,128)} %all-reduce.2.cloned.1.call-done) | copy-start | bytes 393220 | tf_op jit(solution)/shard_map/while
  510.6 0.7 copy-start.4
Sparse Core Ops, SparseCore 0:
  9.2 33.2 all-gather.1
  48.2 34.6 all-reduce.1
  126.2 34.2 all-reduce.1
  203.6 34.2 all-reduce.1
  281.0 34.2 all-reduce.1
  358.4 34.2 all-reduce.1
  436.1 34.2 all-reduce.1
where the time goes:
time: 519 us; the launch traced here: 518 us
  other arithmetic  209 us (40%)
  waiting for transfers between devices  190 us (37%)
  matrix products  42.6 us (8%)
  blocking collectives  33.8 us (7%)
  local copies, waits for them, and re-layouts  26.6 us (5%)
  between operations  13.6 us (3%)
    psum x6, waiting for transfers between devices, batch_step(): batch_obs = lax.psum(selected, 'rows')  190 us
    another operation x18, other arithmetic, batch_gains(): factor = jnp.linalg.cholesky(covariance)  74.3 us
    another operation x12, other arithmetic, batch_gains(): jax.scipy.linalg.solve_triangular(factor, middle, lower=True, trans=1)  63.2 us
    another operation x6, other arithmetic, batch_gains(): inverse = jax.scipy.linalg.solve_triangular(shifted, eye_matrix, lower=True)  58.8 us
    psum x1, blocking collectives, shards(): wind_sums = lax.psum(partial_value, 'rows')  21.3 us
    all_gather x1, blocking collectives, shards(): every_obs = lax.all_gather(group_obs, 'obs', axis=0, tiled=True)  12.6 us
    dot_general x12, matrix products, localised(): jnp.dot(deviation, perturb.T, precision=HIGH, preferred_element_type=jnp....  10.5 us
  transfers between devices with their start and end apart: 7, of which 6 were waited for; matrix products, arithmetic and copies ran while one was open for 5% of the time, Pallas kernels for 0%

commit v1 on v0

v1 whole, which is shorter than its diff:
```python
import functools

import jax
import jax.numpy as jnp
from jax import lax
from jax.experimental import pallas as pl
from jax.experimental.pallas import tpu as pltpu
from jax.sharding import PartitionSpec as P

MEMBERS = 256
BATCH = 128
TILE = 256
RADIUS = 8
SUB = 8
F32 = jnp.float32
BF16 = jnp.bfloat16


HIGH = lax.Precision.HIGHEST
VMEM = pl.BlockSpec(memory_space=pltpu.VMEM)


def model_function(east_wind, north_wind, angles):
    speed = jnp.sqrt(east_wind * east_wind + north_wind * north_wind + 1.0)
    cosine = (east_wind * jnp.cos(angles) + north_wind * jnp.sin(angles)) / speed
    return jnp.exp(0.6 * jnp.log(speed)) * (0.7 + 0.4 * cosine + 0.6 * cosine * cosine)


def taper_weight(bins):
    scaled = 1.0 - bins.astype(F32) / RADIUS
    return jnp.where(bins < RADIUS, scaled * scaled, jnp.zeros_like(scaled))


def halves(value):
    high = value.astype(BF16)
    return high, (value - high.astype(F32)).astype(BF16)


def dot3(left, right, dims=(((1,), (0,)), ((), ()))):
    (left_hi, left_lo), (right_hi, right_lo) = left, right
    dot = functools.partial(lax.dot_general, dimension_numbers=dims, preferred_element_type=F32)
    return dot(left_hi, right_hi) + (dot(left_hi, right_lo) + dot(left_lo, right_hi))


NT = (((1,), (1,)), ((), ()))
TN = (((0,), (0,)), ((), ()))


def factor_inverses(covariance, root_row):
    blocks = BATCH // SUB
    lane = lax.broadcasted_iota(jnp.int32, (SUB, BATCH), 1)
    sub = lax.broadcasted_iota(jnp.int32, (SUB, BATCH), 0)
    work = [covariance[SUB * i : SUB * (i + 1), :] for i in range(blocks)]
    second = [(lane == sub + SUB * i).astype(F32) for i in range(blocks)]
    scales = []
    for j in range(BATCH):
        b, s = divmod(j, SUB)
        at_lane = lane == j
        row = jnp.broadcast_to(work[b][s : s + 1, :], (SUB, BATCH))
        pivot = jnp.broadcast_to(work[b][s : s + 1, j : j + 1], (SUB, BATCH))
        inv_root = lax.rsqrt(pivot)
        inv = inv_root * inv_root
        scaled = jnp.where(at_lane, inv, row * inv)
        diag = pivot * inv_root + jnp.broadcast_to(root_row[:, j : j + 1], (SUB, BATCH))
        second_row = jnp.broadcast_to(second[b][s : s + 1, :], (SUB, BATCH)) * (1.0 / diag)
        second_scaled = second_row * inv_root
        for i in range(b, blocks):
            column = jnp.broadcast_to(work[i][:, j : j + 1], (SUB, BATCH))
            if i == b:
                below = sub > s
                column = jnp.where(below, column, 0.0)
                cleared = jnp.where(jnp.logical_and(at_lane, below), 0.0, work[i])
                work[i] = cleared - column * scaled
                second[i] = jnp.where(sub == s, second_row, second[i] - column * second_scaled)
            else:
                work[i] = jnp.where(at_lane, 0.0, work[i]) - column * scaled
                second[i] = second[i] - column * second_scaled
        scales.append(inv_root)
    firsts = []
    for i in range(blocks):
        scale = scales[SUB * i]
        for s in range(1, SUB):
            scale = jnp.where(sub == s, scales[SUB * i + s], scale)
        diagonal = lane == sub + SUB * i
        unit = jnp.where(diagonal, 1.0, jnp.where(lane < sub + SUB * i, work[i], 0.0))
        firsts.append(unit * scale)
    return jnp.concatenate(firsts, 0), jnp.concatenate(second, 0)


def filter_kernel(
    state_ref, obs_ref, taper_ref, tile_ref, given_ref, order_ref, out_ref, held, weights, picked_given
):
    nobs = obs_ref.shape[0]
    batches = nobs // BATCH
    tiles_dev = tile_ref.shape[0]
    index = lax.broadcasted_iota(jnp.int32, (BATCH, nobs), 1)
    dot = functools.partial(jnp.dot, preferred_element_type=F32)

    def arrange(num, carry):
        rows = pl.ds(pl.multiple_of(num * BATCH, BATCH), BATCH)
        select = (order_ref[rows, :] == index).astype(F32).astype(BF16)
        value = obs_ref[...]
        high, rest = halves(value)
        low = (value - high.astype(F32) - rest.astype(F32)).astype(BF16)
        held[rows, :] = dot(select, high) + (dot(select, rest) + dot(select, low))
        given = given_ref[...]
        high, rest = halves(given)
        low = (given - high.astype(F32) - rest.astype(F32)).astype(BF16)
        picked_given[rows, :] = dot(select, high) + (dot(select, rest) + dot(select, low))
        weights[rows, :] = dot(select, taper_ref[...].astype(BF16))
        return carry

    lax.fori_loop(0, batches, arrange, 0)
    out_ref[...] = state_ref[...]
    eye = lax.broadcasted_iota(jnp.int32, (BATCH, BATCH), 0) == lax.broadcasted_iota(
        jnp.int32, (BATCH, BATCH), 1
    )

    def batch_step(num, carry):
        rows = pl.ds(pl.multiple_of(num * BATCH, BATCH), BATCH)
        batch_obs = held[rows, :]
        row_mean = jnp.mean(batch_obs, axis=1, keepdims=True)
        perturb = batch_obs - row_mean
        given = picked_given[rows, :]
        innov = given[:, 0:1] - row_mean
        variance = given[:, 1:2]
        root_row = jnp.sum(jnp.where(eye, jnp.sqrt(variance), 0.0), axis=0, keepdims=True)
        split = halves(perturb)
        scaled = halves(perturb * (1.0 / (MEMBERS - 1)))
        covariance = dot3(split, scaled, NT) + jnp.where(eye, variance, 0.0)
        first, second = factor_inverses(covariance, root_row)
        first = halves(first)
        middle = dot3(first, halves(jnp.broadcast_to(innov, (BATCH, MEMBERS)))) - dot3(
            halves(second), split
        )
        change = halves(dot3(first, halves(middle), TN))

        def update(ref, place, weight):
            value = ref[place, :]
            product = dot3(halves(value), scaled, NT) * weight
            ref[place, :] = value + dot3(halves(product), change)

        def update_obs(other, inner):
            place = pl.ds(pl.multiple_of(other * BATCH, BATCH), BATCH)
            update(held, place, weights[place, rows])
            return inner

        lax.fori_loop(num + 1, batches, update_obs, 0)
        for tile in range(tiles_dev):
            update(out_ref, pl.ds(tile * TILE, TILE), tile_ref[tile : tile + 1, rows])
        return carry

    lax.fori_loop(0, batches, batch_step, 0)


def filter_all(state, every_obs, taper, tile_taper, given, order_column):
    nobs = every_obs.shape[0]
    return pl.pallas_call(
        filter_kernel,
        out_shape=jax.ShapeDtypeStruct(state.shape, F32),
        in_specs=[VMEM] * 6,
        out_specs=VMEM,
        scratch_shapes=[
            pltpu.VMEM((nobs, MEMBERS), F32),
            pltpu.VMEM((nobs, nobs), F32),
            pltpu.VMEM((nobs, given.shape[1]), F32),
        ],
        compiler_params=pltpu.CompilerParams(vmem_limit_bytes=48 * 1024 * 1024),
    )(state, every_obs, taper, tile_taper, given, order_column)


def shards(state, foot_tiles, foot_weight, azimuth, obs_value, obs_var, tile_bin, obs_bin, order):
    tiles_dev = state.shape[0] // TILE
    half_tile = TILE // 2
    foot_count = foot_tiles.shape[0]
    row_index = lax.axis_index("rows")
    local_tile = foot_tiles - row_index * tiles_dev
    onehot = (
        local_tile[:, :, None] == jnp.arange(tiles_dev, dtype=jnp.int32)[None, None, :]
    ).astype(F32)
    coefficients = jnp.einsum("ftq,ftc->fqc", onehot, foot_weight, precision=HIGH)
    partial_value = jnp.einsum(
        "fqhc,qhcm->fhm",
        coefficients.reshape(foot_count, tiles_dev, 2, half_tile),
        state.reshape(tiles_dev, 2, half_tile, MEMBERS),
        precision=HIGH,
    )
    sorter = (jnp.arange(order.shape[0], dtype=jnp.int32)[:, None] == order[None, :]).astype(BF16)
    own_taper = jnp.dot(taper_weight(obs_bin).astype(BF16), sorter, preferred_element_type=F32)
    tile_taper = jnp.dot(taper_weight(tile_bin).astype(BF16), sorter, preferred_element_type=F32)
    taper = lax.all_gather(own_taper, "obs", axis=0, tiled=True)
    wind_sums = lax.psum(partial_value, "rows")
    angles = azimuth.reshape(foot_count, 4)
    group_obs = model_function(
        wind_sums[:, 0, None, :], wind_sums[:, 1, None, :], angles[:, :, None]
    ).reshape(foot_count * 4, MEMBERS)
    every_obs = lax.all_gather(group_obs, "obs", axis=0, tiled=True)
    given = jnp.stack([obs_value, obs_var], axis=1)
    return filter_all(state, every_obs, taper, tile_taper, given, order[:, None])


def solution(mesh):
    return jax.shard_map(
        shards,
        mesh=mesh,
        in_specs=(
            P(("obs", "rows"), None),
            P("obs", None),
            P("obs", None, None),
            P("obs"),
            P(),
            P(),
            P(("obs", "rows"), None),
            P("obs", None),
            P(),
        ),
        out_specs=P(("obs", "rows"), None),
        check_vma=False,
    )
```

time: 519 us -> 179 us (0.34)
  other arithmetic: 209 us -> 0.83 us
  waiting for transfers between devices: 190 us -> 0.02 us
  Pallas kernels: 0 us -> 125 us
  matrix products: 42.6 us -> 3.41 us
  local copies, waits for them, and re-layouts: 26.6 us -> 4.51 us
    another operation x42 -> x1, other arithmetic: 197 us -> 0.01 us  [shards(): given = jnp.stack([obs_value, obs_var], axis=1)]
    psum x6 -> x0, waiting for transfers between devices: 190 us -> none  [batch_step(): batch_obs = lax.psum(selected, 'rows')]
    pallas_call x0 -> x1, Pallas kernels: none -> 125 us  [filter_all(): pl.pallas_call(filter_kernel, out_shape=jax.ShapeDtypeStruct(state.shape,...]
    dot_general x60 -> x2, matrix products: 37 us -> 2.95 us  [the longest x1 2.44 us: shards(): jnp.dot(taper_weight(obs_bin).astype(BF16), sorter, preferred_element_typ...]
    gather x30 -> x0, local copies, waits for them, and re-layouts: 22.5 us -> none  [the longest x6 5.83 us: batch_step(): obs_var[picked]]
    reduce_sum x8 -> x0, other arithmetic: 6.67 us -> none  [the longest x6 6.45 us: batch_gains(): row_mean = jnp.mean(batch_obs, axis=1)]
  transfers between devices with their start and end apart: 7 -> 1, of which waited for: 6 -> 0; matrix products, arithmetic and copies ran while one was open for 5% -> 3% of each run, Pallas kernels for 0% -> 0%
where the time goes in v1:
time: 179 us
  Pallas kernels  125 us (70%)
  blocking collectives  32.2 us (18%)
  between operations  13.6 us (8%)
  local copies, waits for them, and re-layouts  4.51 us (3%)
  matrix products  3.41 us (2%)
    pallas_call x1, Pallas kernels, filter_all(): pl.pallas_call(filter_kernel, out_shape=jax.ShapeDtypeStruct(state.shape,...  125 us
    psum x1, blocking collectives, shards(): wind_sums = lax.psum(partial_value, 'rows')  21.3 us
    all_gather x1, blocking collectives, shards(): every_obs = lax.all_gather(group_obs, 'obs', axis=0, tiled=True)  10.9 us
  transfers between devices with their start and end apart: 1, of which 0 were waited for; matrix products, arithmetic and copies ran while one was open for 3% of the time, Pallas kernels for 0%

profile of v1, /device:TPU:0, one launch (start us, length us, event | category | flops | bytes accessed | tf_op | source)
XLA Modules:
  0.0 179.1 jit_solution(4374376656614661667)
XLA Ops:
  6.5 0.0 copy-start
  6.5 0.0 copy-start.2
  6.5 0.0 all-gather.2.cloned.1.call-start
  6.5 2.4 %fusion.1 = f32[96,768]{1,0:T(8,128)} fusion(s32[768]{0:T(1024)} %param.17, s32[96,768]{1,0:T(8,128)} %param.16), kind=kOutput, calls=%fused_computation.2 | convolution fusion | flops 114352128 | bytes 592896 | tf_op jit(solution)/shard_map/dot_general | solution.py:189
  9.0 0.0 all-gather.2.cloned.1.call-update
  9.0 0.9 broadcast_in_dim.15.order_ref
  9.9 0.7 stack.9
  10.6 0.7 stack.10
  11.3 0.7 fusion.19
  12.0 0.1 copy.17
  12.1 0.0 copy-done
  12.1 0.2 fusion.33
  12.3 0.0 copy-done.2
  12.3 0.2 convolution_bitcast_fusion
  12.6 21.3 %psum.7 = f32[24,2,256]{2,0,1:T(8,128)S(1)} all-reduce(f32[24,2,256]{2,0,1:T(8,128)S(1)} %convolution_bitcast_fusion), channel_id=1, replica_groups=mesh['obs'=8,'rows'=4] {'rows'}, use_global_device_ids=true, to_apply=%region_0.1 | all-reduce | flops 12288 | bytes 98304 | tf_op jit(solution)/shard_map/psum | solution.py:192
  34.2 0.2 copy.15.given_ref
  34.4 0.0 copy-done.5
  34.4 0.1 fusion.9
  34.5 10.9 %all_gather.6.obs_ref = f32[768,256]{1,0:T(8,128)S(1)} all-gather(f32[96,256]{1,0:T(8,128)S(1)} %fusion.9), channel_id=1, replica_groups=mesh['obs'=8,'rows'=4] {'obs'}, dimensions={0}, use_global_device_ids=true | all-gather | bytes 884736 | tf_op jit(solution)/shard_map/all_gather | solution.py:197
  45.5 0.0 copy-done.3
  45.5 0.0 copy-done.4
  45.5 0.5 fusion.tile_ref
  46.0 1.7 copy-done.1
  47.6 124.6 %shard_map.91 = f32[256,256]{1,0:T(8,128)} custom-call(f32[256,256]{1,0:T(8,128)S(1)} %copy-done.2, f32[768,256]{1,0:T(8,128)S(1)} %all_gather.6.obs_ref, f32[768,768]{1,0:T(8,128)S(1)} %copy-done.1, f32[1,768]{1,0:T(1,128)S(1)} %fusion.tile_ref, f32[768,2]{1,0:T(8,128)S(1)} %copy.15.given_ref, s32[768,1]{1,0:T(8,128)S(1)} %broadcast_in_dim.15.order_ref), custom_call_target="tpu_custom_call" | custom-call | tf_op jit(solution)/shard_map/pallas_call | solution.py:158
  (16 shorter events, 0.3 us)
Async XLA Ops:
  6.5 5.6 %copy-start = (f32[24,4,256]{2,1,0:T(4,128)S(1)}, f32[24,4,256]{2,1,0:T(4,128)}, u32[]{:S(2)}) copy-start(f32[24,4,256]{2,1,0:T(4,128)} %param.11) | copy-start | bytes 294916
  6.5 5.8 %copy-start.2 = (f32[256,256]{1,0:T(8,128)S(1)}, f32[256,256]{1,0:T(8,128)}, u32[]{:S(2)}) copy-start(f32[256,256]{1,0:T(8,128)} %state_ref.1) | copy-start | bytes 786436
  6.5 27.8 %copy-start.5 = (f32[96]{0:T(128)S(1)}, f32[96]{0:T(128)}, u32[]{:S(2)}) copy-start(f32[96]{0:T(128)} %param.12) | copy-start | bytes 1156
  6.5 39.4 %all-gather.2.cloned.1.call-start = ((), (), s32[]{:S(2)}) async-start(), calls=%async_computation | async-start | bytes 2654208 | tf_op jit(solution)/shard_map/all_gather | solution.py:191
  9.0 36.5 %copy-start.3 = (s32[768]{0:T(1024)S(1)}, s32[768]{0:T(1024)}, u32[]{:S(2)}) copy-start(s32[768]{0:T(1024)} %param.17) | copy-start | bytes 9220
  9.0 36.5 %copy-start.4 = (s32[1,768]{1,0:T(1,128)S(1)}, s32[1,768]{1,0:T(1,128)}, u32[]{:S(2)}) copy-start(s32[1,768]{1,0:T(1,128)} %param.15) | copy-start | bytes 9220
  46.0 1.7 copy-start.1
Sparse Core Ops, SparseCore 0:
  9.2 31.9 all-gather.1

commit v2 on v1

--- a/solution.py
+++ b/solution.py
@@ -52,39 +52,49 @@
     sub = lax.broadcasted_iota(jnp.int32, (SUB, BATCH), 0)
     work = [covariance[SUB * i : SUB * (i + 1), :] for i in range(blocks)]
     second = [(lane == sub + SUB * i).astype(F32) for i in range(blocks)]
-    scales = []
-    for j in range(BATCH):
-        b, s = divmod(j, SUB)
-        at_lane = lane == j
-        row = jnp.broadcast_to(work[b][s : s + 1, :], (SUB, BATCH))
-        pivot = jnp.broadcast_to(work[b][s : s + 1, j : j + 1], (SUB, BATCH))
-        inv_root = lax.rsqrt(pivot)
-        inv = inv_root * inv_root
-        scaled = jnp.where(at_lane, inv, row * inv)
-        diag = pivot * inv_root + jnp.broadcast_to(root_row[:, j : j + 1], (SUB, BATCH))
-        second_row = jnp.broadcast_to(second[b][s : s + 1, :], (SUB, BATCH)) * (1.0 / diag)
-        second_scaled = second_row * inv_root
-        for i in range(b, blocks):
-            column = jnp.broadcast_to(work[i][:, j : j + 1], (SUB, BATCH))
-            if i == b:
-                below = sub > s
-                column = jnp.where(below, column, 0.0)
-                cleared = jnp.where(jnp.logical_and(at_lane, below), 0.0, work[i])
-                work[i] = cleared - column * scaled
-                second[i] = jnp.where(sub == s, second_row, second[i] - column * second_scaled)
-            else:
-                work[i] = jnp.where(at_lane, 0.0, work[i]) - column * scaled
-                second[i] = second[i] - column * second_scaled
-        scales.append(inv_root)
-    firsts = []
-    for i in range(blocks):
-        scale = scales[SUB * i]
-        for s in range(1, SUB):
-            scale = jnp.where(sub == s, scales[SUB * i + s], scale)
-        diagonal = lane == sub + SUB * i
-        unit = jnp.where(diagonal, 1.0, jnp.where(lane < sub + SUB * i, work[i], 0.0))
-        firsts.append(unit * scale)
-    return jnp.concatenate(firsts, 0), jnp.concatenate(second, 0)
+
+    def across(value, column):
+        return jnp.broadcast_to(value[:, column : column + 1], (SUB, BATCH))
+
+    def down(value, row):
+        return jnp.broadcast_to(value[row : row + 1, :], (SUB, BATCH))
+
+    for b in range(blocks):
+        base = SUB * b
+        inside = jnp.logical_and(lane >= base, lane < base + SUB)
+        columns = [across(work[b], base + k) for k in range(SUB)]
+        solved = jnp.where(inside, (lane == sub + base).astype(F32), work[b])
+        forward, own, scale = solved, second[b], jnp.zeros((SUB, BATCH), F32)
+        transposed = [jnp.zeros((SUB, BATCH), F32) for _ in range(SUB)]
+        for k in range(SUB):
+            pivot = down(columns[k], k)
+            inv_root = lax.rsqrt(pivot)
+            inv = inv_root * inv_root
+            other, here = sub != k, sub == k
+            for m in range(k + 1, SUB):
+                ratio = down(columns[m], k) * inv
+                columns[m] = jnp.where(other, columns[m] - columns[k] * ratio, ratio)
+                transposed[m] = jnp.where(here, ratio, transposed[m])
+            row = down(solved, k) * inv
+            solved = jnp.where(other, solved - columns[k] * row, row)
+            below = jnp.where(sub > k, columns[k], 0.0)
+            forward = forward - below * (down(forward, k) * inv)
+            row = down(own, k) * (1.0 / (pivot * inv_root + across(root_row, base + k)))
+            own = jnp.where(here, row, own - below * (inv_root * row))
+            scale = jnp.where(here, inv_root, scale)
+        spread = own * scale
+        for m in range(SUB - 1, 0, -1):
+            spread = spread - transposed[m] * down(spread, m)
+        for i in range(b + 1, blocks):
+            panel = [across(work[i], base + k) for k in range(SUB)]
+            value, extra = jnp.where(inside, 0.0, work[i]), second[i]
+            for k in range(SUB):
+                value = value - panel[k] * down(solved, k)
+                extra = extra - panel[k] * down(spread, k)
+            work[i], second[i] = value, extra
+        work[b] = jnp.where(lane <= sub + base, forward * scale, 0.0)
+        second[b] = own
+    return jnp.concatenate(work, 0), jnp.concatenate(second, 0)
 
 
 def filter_kernel(

time: 179 us -> 104 us (0.58)
  Pallas kernels: 125 us -> 49.1 us
    pallas_call x1, Pallas kernels: 125 us -> 49.1 us  [filter_all(): pl.pallas_call(filter_kernel, out_shape=jax.ShapeDtypeStruct(state.shape,...]
  transfers between devices with their start and end apart: 1 -> 1, of which waited for: 0 -> 0; matrix products, arithmetic and copies ran while one was open for 3% -> 4% of each run, Pallas kernels for 0% -> 0%
where the time goes in v2:
time: 104 us
  Pallas kernels  49.1 us (47%)
  blocking collectives  32.2 us (31%)
  between operations  13.6 us (13%)
  local copies, waits for them, and re-layouts  4.51 us (4%)
  matrix products  3.41 us (3%)
    pallas_call x1, Pallas kernels, filter_all(): pl.pallas_call(filter_kernel, out_shape=jax.ShapeDtypeStruct(state.shape,...  49.1 us
    psum x1, blocking collectives, shards(): wind_sums = lax.psum(partial_value, 'rows')  21.3 us
    all_gather x1, blocking collectives, shards(): every_obs = lax.all_gather(group_obs, 'obs', axis=0, tiled=True)  10.9 us
    dot_general x1, matrix products, shards(): jnp.dot(taper_weight(obs_bin).astype(BF16), sorter, preferred_element_typ...  2.44 us
  transfers between devices with their start and end apart: 1, of which 0 were waited for; matrix products, arithmetic and copies ran while one was open for 4% of the time, Pallas kernels for 0%

profile of v2, /device:TPU:0, one launch (start us, length us, event | category | flops | bytes accessed | tf_op | source)
XLA Modules:
  0.0 103.6 jit_solution(12736609693949147599)
XLA Ops:
  6.5 0.0 copy-start
  6.5 0.0 copy-start.2
  6.5 0.0 all-gather.2.cloned.1.call-start
  6.5 2.4 %fusion.1 = f32[96,768]{1,0:T(8,128)} fusion(s32[768]{0:T(1024)} %param.17, s32[96,768]{1,0:T(8,128)} %param.16), kind=kOutput, calls=%fused_computation.2 | convolution fusion | flops 114352128 | bytes 592896 | tf_op jit(solution)/shard_map/dot_general | solution.py:199
  9.0 0.0 all-gather.2.cloned.1.call-update
  9.0 0.9 broadcast_in_dim.15.order_ref
  9.9 0.7 stack.9
  10.6 0.7 stack.10
  11.3 0.7 fusion.19
  12.0 0.1 copy.17
  12.1 0.0 copy-done
  12.1 0.2 fusion.33
  12.3 0.0 copy-done.2
  12.3 0.2 convolution_bitcast_fusion
  12.6 21.3 %psum.7 = f32[24,2,256]{2,0,1:T(8,128)S(1)} all-reduce(f32[24,2,256]{2,0,1:T(8,128)S(1)} %convolution_bitcast_fusion), channel_id=1, replica_groups=mesh['obs'=8,'rows'=4] {'rows'}, use_global_device_ids=true, to_apply=%region_0.1 | all-reduce | flops 12288 | bytes 98304 | tf_op jit(solution)/shard_map/psum | solution.py:202
  34.2 0.2 copy.15.given_ref
  34.4 0.0 copy-done.5
  34.4 0.1 fusion.9
  34.5 10.9 %all_gather.6.obs_ref = f32[768,256]{1,0:T(8,128)S(1)} all-gather(f32[96,256]{1,0:T(8,128)S(1)} %fusion.9), channel_id=1, replica_groups=mesh['obs'=8,'rows'=4] {'obs'}, dimensions={0}, use_global_device_ids=true | all-gather | bytes 884736 | tf_op jit(solution)/shard_map/all_gather | solution.py:207
  45.5 0.0 copy-done.3
  45.5 0.0 copy-done.4
  45.5 0.5 fusion.tile_ref
  46.0 1.7 %copy-done.1 = f32[768,768]{1,0:T(8,128)S(1)} copy-done((f32[768,768]{1,0:T(8,128)S(1)}, f32[768,768]{1,0:T(8,128)}, u32[]{:S(2)}) %copy-start.1) | copy-done | bytes 2359320
  47.6 49.1 %shard_map.91 = f32[256,256]{1,0:T(8,128)} custom-call(f32[256,256]{1,0:T(8,128)S(1)} %copy-done.2, f32[768,256]{1,0:T(8,128)S(1)} %all_gather.6.obs_ref, f32[768,768]{1,0:T(8,128)S(1)} %copy-done.1, f32[1,768]{1,0:T(1,128)S(1)} %fusion.tile_ref, f32[768,2]{1,0:T(8,128)S(1)} %copy.15.given_ref, s32[768,1]{1,0:T(8,128)S(1)} %broadcast_in_dim.15.order_ref), custom_call_target="tpu_custom_call" | custom-call | tf_op jit(solution)/shard_map/pallas_call | solution.py:168
  (16 shorter events, 0.3 us)
Async XLA Ops:
  6.5 5.6 %copy-start = (f32[24,4,256]{2,1,0:T(4,128)S(1)}, f32[24,4,256]{2,1,0:T(4,128)}, u32[]{:S(2)}) copy-start(f32[24,4,256]{2,1,0:T(4,128)} %param.11) | copy-start | bytes 294916
  6.5 5.8 %copy-start.2 = (f32[256,256]{1,0:T(8,128)S(1)}, f32[256,256]{1,0:T(8,128)}, u32[]{:S(2)}) copy-start(f32[256,256]{1,0:T(8,128)} %state_ref.1) | copy-start | bytes 786436
  6.5 27.8 %copy-start.5 = (f32[96]{0:T(128)S(1)}, f32[96]{0:T(128)}, u32[]{:S(2)}) copy-start(f32[96]{0:T(128)} %param.12) | copy-start | bytes 1156
  6.5 39.4 %all-gather.2.cloned.1.call-start = ((), (), s32[]{:S(2)}) async-start(), calls=%async_computation | async-start | bytes 2654208 | tf_op jit(solution)/shard_map/all_gather | solution.py:201
  9.0 36.5 %copy-start.3 = (s32[768]{0:T(1024)S(1)}, s32[768]{0:T(1024)}, u32[]{:S(2)}) copy-start(s32[768]{0:T(1024)} %param.17) | copy-start | bytes 9220
  9.0 36.5 %copy-start.4 = (s32[1,768]{1,0:T(1,128)S(1)}, s32[1,768]{1,0:T(1,128)}, u32[]{:S(2)}) copy-start(s32[1,768]{1,0:T(1,128)} %param.15) | copy-start | bytes 9220
  46.0 1.7 %copy-start.1 = (f32[768,768]{1,0:T(8,128)S(1)}, f32[768,768]{1,0:T(8,128)}, u32[]{:S(2)}) copy-start(f32[768,768]{1,0:T(8,128)} %all-gather.2.cloned.1.call-done.taper_ref) | copy-start | bytes 7077892
Sparse Core Ops, SparseCore 0:
  9.2 31.9 all-gather.1

commit v3 on v2

--- a/solution.py
+++ b/solution.py
@@ -17,12 +17,13 @@
 
 
 HIGH = lax.Precision.HIGHEST
+MESH = pl.DeviceIdType.MESH
 VMEM = pl.BlockSpec(memory_space=pltpu.VMEM)
 
 
-def model_function(east_wind, north_wind, angles):
+def model_function(east_wind, north_wind, cosines, sines):
     speed = jnp.sqrt(east_wind * east_wind + north_wind * north_wind + 1.0)
-    cosine = (east_wind * jnp.cos(angles) + north_wind * jnp.sin(angles)) / speed
+    cosine = (east_wind * cosines + north_wind * sines) / speed
     return jnp.exp(0.6 * jnp.log(speed)) * (0.7 + 0.4 * cosine + 0.6 * cosine * cosine)
 
 
@@ -98,7 +99,7 @@
 
 
 def filter_kernel(
-    state_ref, obs_ref, taper_ref, tile_ref, given_ref, order_ref, out_ref, held, weights, picked_given
+    group_size, state_ref, obs_ref, taper_ref, tile_ref, given_ref, order_ref, order_row_ref, out_ref, held, weights, picked_given
 ):
     nobs = obs_ref.shape[0]
     batches = nobs // BATCH
@@ -106,18 +107,26 @@
     index = lax.broadcasted_iota(jnp.int32, (BATCH, nobs), 1)
     dot = functools.partial(jnp.dot, preferred_element_type=F32)
 
+    lane = lax.broadcasted_iota(jnp.int32, (BATCH, BATCH), 1)
+    before = lane < lax.broadcasted_iota(jnp.int32, (BATCH, BATCH), 0)
+
+    def pick(select, value):
+        high, rest = halves(value)
+        low = (value - high.astype(F32) - rest.astype(F32)).astype(BF16)
+        return dot(select, high) + (dot(select, rest) + dot(select, low))
+
     def arrange(num, carry):
         rows = pl.ds(pl.multiple_of(num * BATCH, BATCH), BATCH)
-        select = (order_ref[rows, :] == index).astype(F32).astype(BF16)
-        value = obs_ref[...]
-        high, rest = halves(value)
-        low = (value - high.astype(F32) - rest.astype(F32)).astype(BF16)
-        held[rows, :] = dot(select, high) + (dot(select, rest) + dot(select, low))
-        given = given_ref[...]
-        high, rest = halves(given)
-        low = (given - high.astype(F32) - rest.astype(F32)).astype(BF16)
-        picked_given[rows, :] = dot(select, high) + (dot(select, rest) + dot(select, low))
-        weights[rows, :] = dot(select, taper_ref[...].astype(BF16))
+        wanted = order_ref[rows, :]
+        select = (wanted == index).astype(F32).astype(BF16)
+        picked_given[rows, :] = pick(select, given_ref[...])
+        group = wanted // group_size
+        same = jnp.logical_and(before, group == order_row_ref[:, rows] // group_size)
+        earlier = jnp.sum(same.astype(F32), axis=1, keepdims=True).astype(jnp.int32)
+        place = group * (group_size // batches) + earlier
+        select = (place == lane).astype(F32).astype(BF16)
+        held[rows, :] = pick(select, obs_ref[rows, :])
+        weights[rows, :] = dot(select, taper_ref[rows, :].astype(BF16))
         return carry
 
     lax.fori_loop(0, batches, arrange, 0)
@@ -163,12 +172,12 @@
     lax.fori_loop(0, batches, batch_step, 0)
 
 
-def filter_all(state, every_obs, taper, tile_taper, given, order_column):
+def filter_all(state, every_obs, taper, tile_taper, given, order, group_size):
     nobs = every_obs.shape[0]
     return pl.pallas_call(
-        filter_kernel,
+        functools.partial(filter_kernel, group_size),
         out_shape=jax.ShapeDtypeStruct(state.shape, F32),
-        in_specs=[VMEM] * 6,
+        in_specs=[VMEM] * 7,
         out_specs=VMEM,
         scratch_shapes=[
             pltpu.VMEM((nobs, MEMBERS), F32),
@@ -176,37 +185,152 @@
             pltpu.VMEM((nobs, given.shape[1]), F32),
         ],
         compiler_params=pltpu.CompilerParams(vmem_limit_bytes=48 * 1024 * 1024),
-    )(state, every_obs, taper, tile_taper, given, order_column)
+    )(state, every_obs, taper, tile_taper, given, order[:, None], order[None, :])
+
+
+def exchange_kernel(
+    groups, layers, state_ref, tiles_ref, weight_ref, cos_ref, sin_ref, order_ref, bins_ref, tile_bin_ref,
+    obs_out, taper_out, tile_out, own_sums, sums, own_obs, own_taper,
+    sum_send, sum_recv, obs_send, obs_recv, taper_send, taper_recv,
+):
+    me, layer = lax.axis_index("obs"), lax.axis_index("rows")
+    feet, batches, per = tiles_ref.shape[0], own_obs.shape[0], own_obs.shape[1]
+    count, nobs = bins_ref.shape
+    tiles_dev, half = tile_bin_ref.shape[0], TILE // 2
+    barrier = pltpu.get_barrier_semaphore()
+    for k in range(1, groups):
+        pl.semaphore_signal(barrier, inc=1, device_id={"obs": lax.rem(me + k, groups)}, device_id_type=MESH)
+    for k in range(1, layers):
+        pl.semaphore_signal(barrier, inc=1, device_id={"rows": lax.rem(layer + k, layers)}, device_id_type=MESH)
+
+    partial = [jnp.zeros((feet, MEMBERS), F32) for _ in range(2)]
+    for tile in range(tiles_dev):
+        number = layer * tiles_dev + tile
+        factor = jnp.zeros((feet, TILE), F32)
+        for t in range(tiles_ref.shape[1]):
+            factor = factor + jnp.where(tiles_ref[:, t : t + 1] == number, weight_ref[:, t, :], 0.0)
+        for h in range(2):
+            partial[h] = partial[h] + jnp.dot(
+                factor[:, h * half : (h + 1) * half],
+                state_ref[pl.ds(tile * TILE + h * half, half), :],
+                precision=HIGH,
+                preferred_element_type=F32,
+            )
+    for h in range(2):
+        own_sums[h] = partial[h]
+    pl.semaphore_wait(barrier, groups + layers - 2)
+
+    sum_copies = []
+    for k in range(1, layers):
+        copy = pltpu.make_async_remote_copy(
+            own_sums, sums.at[k], sum_send.at[k], sum_recv.at[k],
+            device_id={"rows": lax.rem(layer + k, layers)}, device_id_type=MESH,
+        )
+        copy.start()
+        sum_copies.append(copy)
+
+    order = order_ref[...]
+    base = me * count
+    steps = lax.broadcasted_iota(jnp.int32, (count, nobs), 1).astype(F32)
+    member = jnp.logical_and(order >= base, order < base + count).astype(F32)
+    local = lax.broadcasted_iota(jnp.int32, (count, 1), 0)
+    column = lax.broadcasted_iota(jnp.int32, (count, count), 1)
+
+    def ranks(ids):
+        at = jnp.sum(jnp.where(order == base + ids, steps, 0.0), axis=1, keepdims=True)
+        rank = jnp.sum(jnp.where(steps < at, member, 0.0), axis=1, keepdims=True)
+        return (rank.astype(jnp.int32) == column).astype(F32)
+
+    sorter = (lax.broadcasted_iota(jnp.int32, (nobs, nobs), 0) == order).astype(F32).astype(BF16)
+    ordered = jnp.dot(taper_weight(bins_ref[...]).astype(BF16), sorter, preferred_element_type=F32)
+    ordered = lax.dot_general(
+        ranks(local).astype(BF16), ordered.astype(BF16), TN, preferred_element_type=F32
+    )
+    for b in range(batches):
+        own_taper[b] = ordered[b * per : (b + 1) * per, :]
+        taper_out[b, me] = ordered[b * per : (b + 1) * per, :]
+    cuts = [(1, 2), (3, batches - 3)]
+    taper_copies = []
+    for k in range(1, groups):
+        for c, (first, length) in enumerate(cuts):
+            wide = pl.ds(0, (first + length - 1) * BATCH)
+            copy = pltpu.make_async_remote_copy(
+                own_taper.at[pl.ds(first, length), :, wide],
+                taper_out.at[pl.ds(first, length), me, :, wide],
+                taper_send.at[k, c], taper_recv.at[k, c],
+                device_id={"obs": lax.rem(me + k, groups)}, device_id_type=MESH,
+            )
+            copy.start()
+            taper_copies.append(copy)
+
+    tile_out[...] = jnp.dot(taper_weight(tile_bin_ref[...]).astype(BF16), sorter, preferred_element_type=F32)
+    chooser = ranks(local % feet * 4 + local // feet)
+    for copy in sum_copies:
+        copy.wait()
+    winds = [own_sums[h] for h in range(2)]
+    for k in range(1, layers):
+        winds = [winds[h] + sums[k, h] for h in range(2)]
+    observed = jnp.concatenate(
+        [
+            model_function(winds[0], winds[1], cos_ref[:, k : k + 1], sin_ref[:, k : k + 1])
+            for k in range(cos_ref.shape[1])
+        ],
+        0,
+    )
+    observed = lax.dot_general(chooser, observed, TN, precision=HIGH, preferred_element_type=F32)
+    for b in range(batches):
+        own_obs[b] = observed[b * per : (b + 1) * per, :]
+        obs_out[b, me] = observed[b * per : (b + 1) * per, :]
+    obs_copies = []
+    for k in range(1, groups):
+        copy = pltpu.make_async_remote_copy(
+            own_obs, obs_out.at[:, me], obs_send.at[k], obs_recv.at[k],
+            device_id={"obs": lax.rem(me + k, groups)}, device_id_type=MESH,
+        )
+        copy.start()
+        obs_copies.append(copy)
+    for copy in taper_copies + obs_copies:
+        copy.wait()
+
+
+def exchange(state, foot_tiles, foot_weight, cosines, sines, order_row, obs_bin, tile_bin):
+    groups, layers = lax.axis_size("obs"), lax.axis_size("rows")
+    count, nobs = obs_bin.shape
+    batches, feet = nobs // BATCH, foot_tiles.shape[0]
+    per = count // batches
+    dma = pltpu.SemaphoreType.DMA
+    return pl.pallas_call(
+        functools.partial(exchange_kernel, groups, layers),
+        out_shape=(
+            jax.ShapeDtypeStruct((batches, groups, per, MEMBERS), F32),
+            jax.ShapeDtypeStruct((batches, groups, per, nobs), F32),
+            jax.ShapeDtypeStruct(tile_bin.shape, F32),
+        ),
+        in_specs=[VMEM] * 8,
+        out_specs=(VMEM, VMEM, VMEM),
+        scratch_shapes=[
+            pltpu.VMEM((2, feet, MEMBERS), F32),
+            pltpu.VMEM((layers, 2, feet, MEMBERS), F32),
+            pltpu.VMEM((batches, per, MEMBERS), F32),
+            pltpu.VMEM((batches, per, nobs), F32),
+            dma((layers,)), dma((layers,)), dma((groups,)), dma((groups,)), dma((groups, 2)), dma((groups, 2)),
+        ],
+        compiler_params=pltpu.CompilerParams(
+            collective_id=0, has_side_effects=True, vmem_limit_bytes=48 * 1024 * 1024
+        ),
+    )(state, foot_tiles, foot_weight, cosines, sines, order_row, obs_bin, tile_bin)
 
 
 def shards(state, foot_tiles, foot_weight, azimuth, obs_value, obs_var, tile_bin, obs_bin, order):
-    tiles_dev = state.shape[0] // TILE
-    half_tile = TILE // 2
-    foot_count = foot_tiles.shape[0]
-    row_index = lax.axis_index("rows")
-    local_tile = foot_tiles - row_index * tiles_dev
-    onehot = (
-        local_tile[:, :, None] == jnp.arange(tiles_dev, dtype=jnp.int32)[None, None, :]
-    ).astype(F32)
-    coefficients = jnp.einsum("ftq,ftc->fqc", onehot, foot_weight, precision=HIGH)
-    partial_value = jnp.einsum(
-        "fqhc,qhcm->fhm",
-        coefficients.reshape(foot_count, tiles_dev, 2, half_tile),
-        state.reshape(tiles_dev, 2, half_tile, MEMBERS),
-        precision=HIGH,
-    )
-    sorter = (jnp.arange(order.shape[0], dtype=jnp.int32)[:, None] == order[None, :]).astype(BF16)
-    own_taper = jnp.dot(taper_weight(obs_bin).astype(BF16), sorter, preferred_element_type=F32)
-    tile_taper = jnp.dot(taper_weight(tile_bin).astype(BF16), sorter, preferred_element_type=F32)
-    taper = lax.all_gather(own_taper, "obs", axis=0, tiled=True)
-    wind_sums = lax.psum(partial_value, "rows")
-    angles = azimuth.reshape(foot_count, 4)
-    group_obs = model_function(
-        wind_sums[:, 0, None, :], wind_sums[:, 1, None, :], angles[:, :, None]
-    ).reshape(foot_count * 4, MEMBERS)
-    every_obs = lax.all_gather(group_obs, "obs", axis=0, tiled=True)
+    angles = azimuth.reshape(foot_tiles.shape[0], -1)
+    every_obs, taper, tile_taper = exchange(
+        state, foot_tiles, foot_weight, jnp.cos(angles), jnp.sin(angles), order[None, :], obs_bin, tile_bin
+    )
+    nobs = order.shape[0]
     given = jnp.stack([obs_value, obs_var], axis=1)
-    return filter_all(state, every_obs, taper, tile_taper, given, order[:, None])
+    return filter_all(
+        state, every_obs.reshape(nobs, MEMBERS), taper.reshape(nobs, nobs), tile_taper, given, order, obs_bin.shape[0]
+    )
 
 
 def solution(mesh):

time: 104 us -> 85.5 us (0.82)
  blocking collectives: 32.2 us -> 0 us
  Pallas kernels: 49.1 us -> 76.5 us
  between operations: 13.6 us -> 0.06 us
  local copies, waits for them, and re-layouts: 4.51 us -> 8.22 us
  matrix products: 3.41 us -> 0 us
    pallas_call x1 -> x2, Pallas kernels: 49.1 us -> 76.5 us  [the longest x1 47.5 us: filter_all(): pl.pallas_call(functools.partial(filter_kernel, group_size), out_shape=ja...]
    psum x1 -> x0, blocking collectives: 21.3 us -> none  [shards(): wind_sums = lax.psum(partial_value, 'rows')]
    all_gather x1 -> x0, blocking collectives: 10.9 us -> none  [shards(): every_obs = lax.all_gather(group_obs, 'obs', axis=0, tiled=True)]
    dot_general x4 -> x0, matrix products: 3.41 us -> none  [the longest x1 2.44 us: shards(): jnp.dot(taper_weight(obs_bin).astype(BF16), sorter, preferred_element_typ...]
    unnamed x12 -> x9, local copies, waits for them, and re-layouts: 1.69 us -> 4.25 us
  transfers between devices with their start and end apart: 1 -> 0, of which waited for: 0 -> 0; matrix products, arithmetic and copies ran while one was open for 4% -> 0% of each run, Pallas kernels for 0% -> 0%
where the time goes in v3:
time: 85.5 us; the launch traced here: 84.8 us
  Pallas kernels  76.5 us (89%)
  local copies, waits for them, and re-layouts  8.22 us (10%)
    pallas_call x1, Pallas kernels, filter_all(): pl.pallas_call(functools.partial(filter_kernel, group_size), out_shape=ja...  47.5 us
    pallas_call x1, Pallas kernels, exchange(): pl.pallas_call(functools.partial(exchange_kernel, groups, layers), out_sh...  29 us
    unnamed x9, local copies, waits for them, and re-layouts  4.25 us

profile of v3, /device:TPU:0, one launch (start us, length us, event | category | flops | bytes accessed | tf_op | source)
XLA Modules:
  0.0 84.8 jit_solution(5676019645628491069)
XLA Ops:
  0.0 0.7 fusion
  0.7 0.7 broadcast_in_dim.7.order_ref.order_row_ref
  1.4 0.7 stack.9
  2.1 0.7 stack.10
  2.8 0.1 sin.6.sin_ref
  2.9 0.1 cos.6.cos_ref
  3.0 0.8 copy.15.tiles_ref
  3.7 0.2 copy.16.given_ref
  3.9 0.8 broadcast_in_dim.9.order_ref
  4.8 0.0 copy-start
  4.8 0.9 %copy-done = f32[256,256]{1,0:T(8,128)S(1)} copy-done((f32[256,256]{1,0:T(8,128)S(1)}, f32[256,256]{1,0:T(8,128)}, u32[]{:S(2)}) %copy-start) | copy-done | bytes 262168
  5.7 0.0 copy-start.1
  5.7 1.0 %copy-done.1 = s32[96,768]{1,0:T(8,128)S(1)} copy-done((s32[96,768]{1,0:T(8,128)S(1)}, s32[96,768]{1,0:T(8,128)}, u32[]{:S(2)}) %copy-start.1) | copy-done | bytes 294936
  6.7 0.0 copy-start.2
  6.7 0.9 %copy-done.2 = f32[24,4,256]{2,1,0:T(4,128)S(1)} copy-done((f32[24,4,256]{2,1,0:T(4,128)S(1)}, f32[24,4,256]{2,1,0:T(4,128)}, u32[]{:S(2)}) %copy-start.2) | copy-done | bytes 98328
  7.6 0.0 copy-start.3
  7.6 0.7 copy-done.3
  8.3 29.0 %shard_map.91 = (f32[6,8,16,256]{3,2,1,0:T(8,128)S(1)}, f32[6,8,16,768]{3,2,1,0:T(8,128)S(1)}, f32[1,768]{1,0:T(1,128)S(1)}) custom-call(f32[256,256]{1,0:T(8,128)S(1)} %copy-done, s32[24,4]{1,0:T(8,128)S(1)} %copy.15.tiles_ref, f32[24,4,256]{2,1,0:T(4,128)S(1)} %copy-done.2, f32[24,4]{1,0:T(8,128)S(1)} %cos.6.cos_ref, f32[24,4]{1,0:T(8,128)S(1)} %sin.6.sin_ref, ...), custom_call_target="tpu_custom_call" | custom-call | tf_op jit(solution)/shard_map/pallas_call | solution.py:302
  37.3 47.5 %shard_map.92 = f32[256,256]{1,0:T(8,128)} custom-call(f32[256,256]{1,0:T(8,128)S(1)} %copy-done, f32[768,256]{1,0:T(8,128)S(1)} %bitcast.3, f32[768,768]{1,0:T(8,128)S(1)} %bitcast.2, f32[1,768]{1,0:T(1,128)S(1)} %get-tuple-element.10.tile_ref, f32[768,2]{1,0:T(8,128)S(1)} %copy.16.given_ref, s32[768,1]{1,0:T(8,128)S(1)} %broadcast_in_dim.9.order_ref, ...), custom_call_target="tpu_custom_call" | custom-call | tf_op jit(solution)/shard_map/pallas_call | solution.py:177
  (1 shorter events, 0.0 us)
Async XLA Ops:
  4.8 1.0 %copy-start = (f32[256,256]{1,0:T(8,128)S(1)}, f32[256,256]{1,0:T(8,128)}, u32[]{:S(2)}) copy-start(f32[256,256]{1,0:T(8,128)} %state_ref.3) | copy-start | bytes 786436
  5.7 1.0 %copy-start.1 = (s32[96,768]{1,0:T(8,128)S(1)}, s32[96,768]{1,0:T(8,128)}, u32[]{:S(2)}) copy-start(s32[96,768]{1,0:T(8,128)} %bins_ref.1) | copy-start | bytes 884740
  6.7 0.9 %copy-start.2 = (f32[24,4,256]{2,1,0:T(4,128)S(1)}, f32[24,4,256]{2,1,0:T(4,128)}, u32[]{:S(2)}) copy-start(f32[24,4,256]{2,1,0:T(4,128)} %weight_ref.1) | copy-start | bytes 294916
  7.6 0.7 copy-start.3

commit v4 on v3

--- a/solution.py
+++ b/solution.py
@@ -249,7 +249,7 @@
     for b in range(batches):
         own_taper[b] = ordered[b * per : (b + 1) * per, :]
         taper_out[b, me] = ordered[b * per : (b + 1) * per, :]
-    cuts = [(1, 2), (3, batches - 3)]
+    cuts = [(b, 1) for b in range(1, batches)]
     taper_copies = []
     for k in range(1, groups):
         for c, (first, length) in enumerate(cuts):
@@ -313,7 +313,7 @@
             pltpu.VMEM((layers, 2, feet, MEMBERS), F32),
             pltpu.VMEM((batches, per, MEMBERS), F32),
             pltpu.VMEM((batches, per, nobs), F32),
-            dma((layers,)), dma((layers,)), dma((groups,)), dma((groups,)), dma((groups, 2)), dma((groups, 2)),
+            dma((layers,)), dma((layers,)), dma((groups,)), dma((groups,)), dma((groups, batches)), dma((groups, batches)),
         ],
         compiler_params=pltpu.CompilerParams(
             collective_id=0, has_side_effects=True, vmem_limit_bytes=48 * 1024 * 1024

time: 85.5 us -> 83.3 us (0.974)
  Pallas kernels: 76.5 us -> 74.2 us
    pallas_call x1, Pallas kernels: 29 us -> 26.8 us  [exchange(): pl.pallas_call(functools.partial(exchange_kernel, groups, layers), out_sh...]
where the time goes in v4:
time: 83.3 us; the launch traced here: 82.5 us
  Pallas kernels  74.2 us (89%)
  local copies, waits for them, and re-layouts  8.22 us (10%)
    pallas_call x1, Pallas kernels, filter_all(): pl.pallas_call(functools.partial(filter_kernel, group_size), out_shape=ja...  47.5 us
    pallas_call x1, Pallas kernels, exchange(): pl.pallas_call(functools.partial(exchange_kernel, groups, layers), out_sh...  26.8 us
    unnamed x9, local copies, waits for them, and re-layouts  4.25 us

profile of v4, /device:TPU:0, one launch (start us, length us, event | category | flops | bytes accessed | tf_op | source)
XLA Modules:
  0.0 82.5 jit_solution(13590236103336431806)
XLA Ops:
  0.0 0.7 fusion
  0.7 0.7 broadcast_in_dim.7.order_ref.order_row_ref
  1.4 0.7 stack.9
  2.1 0.7 stack.10
  2.8 0.1 sin.6.sin_ref
  2.9 0.1 cos.6.cos_ref
  3.0 0.8 copy.15.tiles_ref
  3.7 0.2 copy.16.given_ref
  3.9 0.8 %broadcast_in_dim.9.order_ref = s32[768,1]{1,0:T(8,128)S(1)} reshape(s32[768]{0:T(1024)} %param.17) | data formatting | bytes 6144 | tf_op jit(solution)/shard_map/broadcast_in_dim | solution.py:188
  4.8 0.0 copy-start
  4.8 0.9 %copy-done = f32[256,256]{1,0:T(8,128)S(1)} copy-done((f32[256,256]{1,0:T(8,128)S(1)}, f32[256,256]{1,0:T(8,128)}, u32[]{:S(2)}) %copy-start) | copy-done | bytes 262168
  5.7 0.0 copy-start.1
  5.7 1.0 %copy-done.1 = s32[96,768]{1,0:T(8,128)S(1)} copy-done((s32[96,768]{1,0:T(8,128)S(1)}, s32[96,768]{1,0:T(8,128)}, u32[]{:S(2)}) %copy-start.1) | copy-done | bytes 294936
  6.7 0.0 copy-start.2
  6.7 0.9 %copy-done.2 = f32[24,4,256]{2,1,0:T(4,128)S(1)} copy-done((f32[24,4,256]{2,1,0:T(4,128)S(1)}, f32[24,4,256]{2,1,0:T(4,128)}, u32[]{:S(2)}) %copy-start.2) | copy-done | bytes 98328
  7.6 0.0 copy-start.3
  7.6 0.7 copy-done.3
  8.3 26.8 %shard_map.91 = (f32[6,8,16,256]{3,2,1,0:T(8,128)S(1)}, f32[6,8,16,768]{3,2,1,0:T(8,128)S(1)}, f32[1,768]{1,0:T(1,128)S(1)}) custom-call(f32[256,256]{1,0:T(8,128)S(1)} %copy-done, s32[24,4]{1,0:T(8,128)S(1)} %copy.15.tiles_ref, f32[24,4,256]{2,1,0:T(4,128)S(1)} %copy-done.2, f32[24,4]{1,0:T(8,128)S(1)} %cos.6.cos_ref, f32[24,4]{1,0:T(8,128)S(1)} %sin.6.sin_ref, ...), custom_call_target="tpu_custom_call" | custom-call | tf_op jit(solution)/shard_map/pallas_call | solution.py:302
  35.1 47.5 %shard_map.92 = f32[256,256]{1,0:T(8,128)} custom-call(f32[256,256]{1,0:T(8,128)S(1)} %copy-done, f32[768,256]{1,0:T(8,128)S(1)} %bitcast.3, f32[768,768]{1,0:T(8,128)S(1)} %bitcast.2, f32[1,768]{1,0:T(1,128)S(1)} %get-tuple-element.10.tile_ref, f32[768,2]{1,0:T(8,128)S(1)} %copy.16.given_ref, s32[768,1]{1,0:T(8,128)S(1)} %broadcast_in_dim.9.order_ref, ...), custom_call_target="tpu_custom_call" | custom-call | tf_op jit(solution)/shard_map/pallas_call | solution.py:177
  (1 shorter events, 0.0 us)
Async XLA Ops:
  4.8 1.0 %copy-start = (f32[256,256]{1,0:T(8,128)S(1)}, f32[256,256]{1,0:T(8,128)}, u32[]{:S(2)}) copy-start(f32[256,256]{1,0:T(8,128)} %state_ref.3) | copy-start | bytes 786436
  5.7 1.0 %copy-start.1 = (s32[96,768]{1,0:T(8,128)S(1)}, s32[96,768]{1,0:T(8,128)}, u32[]{:S(2)}) copy-start(s32[96,768]{1,0:T(8,128)} %bins_ref.1) | copy-start | bytes 884740
  6.7 0.9 %copy-start.2 = (f32[24,4,256]{2,1,0:T(4,128)S(1)}, f32[24,4,256]{2,1,0:T(4,128)}, u32[]{:S(2)}) copy-start(f32[24,4,256]{2,1,0:T(4,128)} %weight_ref.1) | copy-start | bytes 294916
  7.6 0.7 copy-start.3
